TPU v7x, 256 devices: a whole 4x4x8 slice. The times are simulated.
256 devices in a mesh: dp: 32 (over x, z), frame: 8 (over y, core).
Axes of the slice: x: 4, y: 4, z: 8, core: 2. Of those that a mesh axis runs over, the one named last changes fastest.
Arguments:
- features: bfloat16 [32, 16, 32, 64, 128], P('dp', 'frame'), may hold values from -6 to 6
- vis_block: int32 [32, 16, 16, 2], P('dp', None, 'frame'), may hold values from 0 to 31
- vis_count: int32 [32, 16, 16], P('dp', None, 'frame'), may hold values from 1 to 2
- query_frame: int32 [32, 256], P('dp'), may hold values from 0 to 15
- query_block: int32 [32, 256], P('dp'), may hold values from 0 to 31
- query_cell: int32 [32, 256], P('dp'), may hold values from 0 to 63
- cotangent: bfloat16 [32, 4, 256, 16], P('dp', None, 'frame')
- w_in: bfloat16 [128, 384], replicated, may hold values from -0.5 to 0.5
- gain: float32 [384], replicated, may hold values from 0.1 to 1.9
- w_qkv: bfloat16 [384, 1152], replicated, may hold values from -0.3125 to 0.3125
- w_out: bfloat16 [384, 384], replicated, may hold values from -0.3125 to 0.3125
- w_head: bfloat16 [4, 384], replicated, may hold values from -0.3125 to 0.3125
Outputs:
- grad_in: float32 [128, 384], replicated
- grad_gain: float32 [384], replicated
- grad_qkv: float32 [384, 1152], replicated
- grad_out: float32 [384, 384], replicated
- grad_head: float32 [4, 384], replicated
Inputs may be any that keep to these rules, and one draw needn't show every extreme that they name: vis_count counts the leading visible slots of vis_block.
All inputs are finite; a program needn't handle non-finite values.
Results may differ from a plain program's by a relative error of at most 0.012.
Values may be sent and summed in bfloat16 or wider, within the bound.
No kernel may reach another device: no remote copies, remote signals or barrier semaphores. Data moves between devices by JAX's collectives and lax.ppermute only.
A program may use at most 64 MiB of HBM per device.

v0:
```python
import jax
import jax.numpy as jnp
from jax import lax
from jax.sharding import PartitionSpec as P

HEADS = 8


def attend(query, keys, values):
    scale = query.shape[-1] ** (-0.5)
    scores = (
        jnp.einsum("nfhd,nghd->nhfg", query.astype(jnp.float32), keys.astype(jnp.float32)) * scale
    )
    probs = jax.nn.softmax(scores, axis=-1).astype(jnp.bfloat16)
    probs = lax.optimization_barrier(probs)
    mixed = jnp.einsum("nhfg,nghd->nfhd", probs.astype(jnp.float32), values.astype(jnp.float32))
    return mixed.astype(jnp.bfloat16)


def inner_rows(left, right):
    return lax.dot_general(
        left, right, (((0,), (0,)), ((), ())), preferred_element_type=jnp.float32
    )


def outer_cols(left, right):
    return lax.dot_general(
        left, right, (((1,), (1,)), ((), ())), preferred_element_type=jnp.float32
    )


def local_grads(corr, cot, w_in, gain, w_qkv, w_out, w_head):
    tracks, frames, width = corr.shape
    total = tracks * frames
    hid = w_in.shape[1]
    head_size = hid // HEADS
    rows = corr.reshape(total, width)
    x_zero = jnp.dot(rows, w_in, preferred_element_type=jnp.float32)
    centred = x_zero - jnp.mean(x_zero, axis=-1, keepdims=True)
    inv_std = lax.rsqrt(jnp.mean(centred * centred, axis=-1, keepdims=True) + 1e-05)
    normed = centred * inv_std
    hidden = (normed * gain).astype(jnp.bfloat16)
    qkv = jnp.dot(hidden, w_qkv, preferred_element_type=jnp.float32).astype(jnp.bfloat16)
    split = qkv.reshape(tracks, frames, 3, HEADS, head_size)
    mixed, backward = jax.vjp(attend, split[:, :, 0], split[:, :, 1], split[:, :, 2])
    mixed = mixed.reshape(total, hid)
    y_out = (x_zero + jnp.dot(mixed, w_out, preferred_element_type=jnp.float32)).astype(
        jnp.bfloat16
    )
    ct_rows = cot.reshape(cot.shape[0], total)
    g_head = jnp.dot(ct_rows, y_out, preferred_element_type=jnp.float32)
    d_y = inner_rows(ct_rows, w_head)
    d_y16 = d_y.astype(jnp.bfloat16)
    g_out = inner_rows(mixed, d_y16)
    d_mixed = outer_cols(d_y16, w_out).astype(jnp.bfloat16)
    d_q, d_k, d_v = backward(d_mixed.reshape(tracks, frames, HEADS, head_size))
    d_qkv = jnp.stack([d_q, d_k, d_v], axis=2).reshape(total, 3 * hid)
    g_qkv = inner_rows(hidden, d_qkv)
    d_hidden = outer_cols(d_qkv, w_qkv)
    g_gain = jnp.sum(d_hidden * normed, axis=0)
    d_norm = d_hidden * gain
    d_x = (
        inv_std
        * (
            d_norm
            - jnp.mean(d_norm, axis=-1, keepdims=True)
            - normed * jnp.mean(d_norm * normed, axis=-1, keepdims=True)
        )
        + d_y
    )
    d_x16 = d_x.astype(jnp.bfloat16)
    g_in = inner_rows(rows, d_x16)
    return (g_in, g_gain, g_qkv, g_out, g_head)


def body(
    features,
    vis_block,
    vis_count,
    query_frame,
    query_block,
    query_cell,
    cotangent,
    w_in,
    gain,
    w_qkv,
    w_out,
    w_head,
):
    feats = features[0]
    fr_dev = feats.shape[0]
    cells = feats.shape[2]
    width = feats.shape[3]
    trk_dev = cotangent.shape[2]
    frame_pos = lax.axis_index("frame")
    frames_q = query_frame[0]
    blocks_q = query_block[0]
    cells_q = query_cell[0]
    local = frames_q - frame_pos * fr_dev
    inside = (local >= 0) & (local < fr_dev)
    picked = feats[jnp.clip(local, 0, fr_dev - 1), blocks_q, cells_q].astype(jnp.float32)
    query = lax.psum_scatter(
        jnp.where(inside[:, None], picked, 0.0).astype(jnp.bfloat16),
        "frame",
        scatter_dimension=0,
        tiled=True,
    )
    groups = vis_block.shape[1]
    slots = vis_block.shape[3]
    frame_ids = jnp.arange(fr_dev, dtype=jnp.int32)[None, :, None]
    patches = feats[frame_ids, vis_block[0]]
    live = jnp.arange(slots, dtype=jnp.int32)[None, None, :] < vis_count[0][:, :, None]
    patches = jnp.where(live[..., None, None], patches, jnp.zeros((), jnp.bfloat16))
    scale = width ** (-0.5)
    outgoing = patches.reshape(groups, fr_dev, slots, cells * width)
    arrived = lax.all_to_all(outgoing, "frame", split_axis=0, concat_axis=1, tiled=True)
    own_groups = arrived.shape[0]
    all_frames = arrived.shape[1]
    arrived = arrived.reshape(own_groups, all_frames, slots, cells, width)
    corr = jnp.einsum(
        "gtc,gfkpc->gtfkp",
        query.reshape(own_groups, -1, width),
        arrived,
        preferred_element_type=jnp.float32,
    )
    corr = (corr * scale).astype(jnp.bfloat16).reshape(trk_dev, all_frames, slots * cells)
    g_in, g_gain, g_qkv, g_out, g_head = local_grads(
        corr, cotangent[0], w_in, gain, w_qkv, w_out, w_head
    )
    s_in, s_gain, s_qkv, s_out, s_head = lax.psum(
        (g_in, g_gain, g_qkv, g_out, g_head), ("dp", "frame")
    )
    return (s_in, s_gain, s_qkv, s_out, s_head)


def solution(mesh):
    in_specs = (
        P("dp", "frame", None, None, None),
        P("dp", None, "frame", None),
        P("dp", None, "frame"),
        P("dp", None),
        P("dp", None),
        P("dp", None),
        P("dp", None, "frame", None),
        P(),
        P(),
        P(),
        P(),
        P(),
    )
    out_specs = (P(), P(), P(), P(), P())
    return jax.shard_map(body, mesh=mesh, in_specs=in_specs, out_specs=out_specs, check_vma=False)
```

profile of v0, /device:TPU:2, one launch (start us, length us, event | category | flops | bytes accessed | tf_op | source)
XLA Modules:
  0.0 383.4 jit_solution(13826835870761128297)
XLA Ops:
  9.7 1.9 broadcast_select_fusion
  11.7 4.5 %all-to-all-start = ((bf16[16,2,2,8192]{3,2,1,0:T(2,128)(2,1)}), bf16[16,2,2,8192]{3,2,1,0:T(2,128)(2,1)}, u32[]{:S(2)}, u32[]{:S(2)}) async-start(bf16[16,2,2,8192]{3,2,1,0:T(2,128)(2,1)} %broadcast_select_fusion), calls=%async_computation.1 | async-start | bytes 2097152 | tf_op jit(solution)/shard_map/all_to_all | solution.py:116
  16.3 1.9 gather_fusion
  23.0 9.2 %all-to-all-done = bf16[16,2,2,8192]{3,2,1,0:T(2,128)(2,1)} async-done(((bf16[16,2,2,8192]{3,2,1,0:T(2,128)(2,1)}), bf16[16,2,2,8192]{3,2,1,0:T(2,128)(2,1)}, u32[]{:S(2)}, u32[]{:S(2)}) %all-to-all-start) | async-done | bytes 1048608 | tf_op jit(solution)/shard_map/all_to_all | solution.py:116
  32.2 3.4 copy.29
  35.6 2.7 reshape.196
  38.3 18.2 %reduce-scatter.2.cloned.1.call-done = bf16[32,128]{1,0:T(8,128)(2,1)} async-done(((bf16[256,128]{1,0:T(8,128)(2,1)}), bf16[32,128]{1,0:T(8,128)(2,1)}) %reduce-scatter.2.cloned.1.call-update) | async-done | bytes 8208 | tf_op jit(solution)/shard_map/reduce_scatter | solution.py:102
  56.5 2.1 fusion.13
  59.5 3.1 convolution_convert_fusion
  62.7 5.3 %reshape.198 = bf16[32,16,3,8,48]{4,3,2,1,0:T(8,128)(2,1)} reshape(bf16[512,1152]{1,0:T(8,128)(2,1)} %convolution_convert_fusion) | data formatting | bytes 2359296 | tf_op jit(solution)/shard_map/reshape | solution.py:44
  67.9 3.7 fusion.40
  71.6 3.8 fusion.42
  75.4 2.3 convolution_convert_fusion.5
  77.8 1.9 fusion.5
  79.8 1.9 fusion.7
  81.7 2.5 fusion.8
  87.2 2.5 copy.39
  89.6 5.0 %reshape.199 = bf16[512,1152]{1,0:T(8,128)(2,1)} reshape(bf16[32,16,3,8,48]{4,3,2,1,0:T(8,128)(2,1)} %copy.39) | data formatting | bytes 2359296 | tf_op jit(solution)/shard_map/reshape | solution.py:57
  94.6 3.3 multiply_reduce_fusion.1
  98.0 1.9 fusion.37
  101.1 2.0 reshape.200
  106.3 74.6 %all-reduce = (f32[384]{0:T(512)}, f32[4,384]{1,0:T(4,128)}) all-reduce(f32[384]{0:T(512)S(1)} %get-tuple-element.5, f32[4,384]{1,0:T(4,128)S(1)} %fusion.14), channel_id=1, replica_groups=mesh['dp'=32,'frame'=8] {'dp','frame'}, use_global_device_ids=true, to_apply=%region_10.11 | all-reduce | flops 1920 | bytes 15360 | tf_op jit(solution)/shard_map/psum | solution.py:130
  180.9 190.4 %all-reduce.4.cloned.1.call-done = (f32[128,384]{1,0:T(8,128)}, f32[384,1152]{1,0:T(8,128)}, f32[384,384]{1,0:T(8,128)}) async-done(((f32[128,384]{1,0:T(8,128)}, f32[384,1152]{1,0:T(8,128)}, f32[384,384]{1,0:T(8,128)}), (f32[128,384]{1,0:T(8,128)}, f32[384,1152]{1,0:T(8,128)}, f32[384,384]{1,0:T(8,128)})) %all-reduce.4.cloned.1.call-update) | async-done | bytes 2555920 | tf_op jit(solution)/shard_map/psum | solution.py:130
  372.9 2.8 copy.86
  (78 shorter events, 18.0 us)
Async XLA Ops:
  7.2 1.2 copy-start
  8.4 1.1 copy-start.17
  9.7 6.5 %copy-start.15 = (s32[1,256]{1,0:T(1,128)S(1)}, s32[1,256]{1,0:T(1,128)}, u32[]{:S(2)}) copy-start(s32[1,256]{1,0:T(1,128)} %param.15) | copy-start | bytes 3076
  9.7 6.5 %copy-start.18 = (s32[1,256]{1,0:T(1,128)S(1)}, s32[1,256]{1,0:T(1,128)}, u32[]{:S(2)}) copy-start(s32[1,256]{1,0:T(1,128)} %param.17) | copy-start | bytes 3076
  9.7 6.5 %copy-start.19 = (s32[1,256]{1,0:T(1,128)S(1)}, s32[1,256]{1,0:T(1,128)}, u32[]{:S(2)}) copy-start(s32[1,256]{1,0:T(1,128)} %param.16) | copy-start | bytes 3076
  9.7 9.3 %copy-start.14 = (bf16[1,4,32,16]{2,3,1,0:T(8,128)(2,1)S(1)}, bf16[1,4,32,16]{2,3,1,0:T(8,128)(2,1)}, u32[]{:S(2)}) copy-start(bf16[1,4,32,16]{2,3,1,0:T(8,128)(2,1)} %param.18) | copy-start | bytes 12292
  9.7 9.5 %copy-start.16 = (bf16[4,384]{1,0:T(4,128)(2,1)S(1)}, bf16[4,384]{1,0:T(4,128)(2,1)}, u32[]{:S(2)}) copy-start(bf16[4,384]{1,0:T(4,128)(2,1)} %param.23) | copy-start | bytes 9220
  11.7 20.5 %all-to-all-start = ((bf16[16,2,2,8192]{3,2,1,0:T(2,128)(2,1)}), bf16[16,2,2,8192]{3,2,1,0:T(2,128)(2,1)}, u32[]{:S(2)}, u32[]{:S(2)}) async-start(bf16[16,2,2,8192]{3,2,1,0:T(2,128)(2,1)} %broadcast_select_fusion), calls=%async_computation.1 | async-start | bytes 2097152 | tf_op jit(solution)/shard_map/all_to_all | solution.py:116
  16.1 4.6 %copy-start.7 = (bf16[384,384]{1,0:T(8,128)(2,1)S(1)}, bf16[384,384]{1,0:T(8,128)(2,1)}, u32[]{:S(2)}) copy-start(bf16[384,384]{1,0:T(8,128)(2,1)} %param.22) | copy-start | bytes 884740
  16.1 40.4 %reduce-scatter.2.cloned.1.call-start = ((), (), s32[]{:S(2)}) async-start(), calls=%async_computation.2 | async-start | bytes 73728 | tf_op jit(solution)/shard_map/reduce_scatter | solution.py:102
  19.0 352.3 %all-reduce.4.cloned.1.call-start = ((), (), s32[]{:S(2)}) async-start(), calls=%async_computation.3 | async-start | bytes 5111808 | tf_op jit(solution)/shard_map/psum | solution.py:130
  35.6 23.4 %copy-start.12 = (bf16[128,384]{1,0:T(8,128)(2,1)S(1)}, bf16[128,384]{1,0:T(8,128)(2,1)}, u32[]{:S(2)}) copy-start(bf16[128,384]{1,0:T(8,128)(2,1)} %param.19) | copy-start | bytes 294916
  38.3 21.2 %copy-start.13 = (f32[384]{0:T(512)S(1)}, f32[384]{0:T(512)}, u32[]{:S(2)}) copy-start(f32[384]{0:T(512)} %param.20) | copy-start | bytes 4612
  75.4 2.4 copy-start.6
  77.8 1.9 copy-start.9
  79.7 1.9 copy-start.8
  81.7 2.5 copy-start.2
  84.2 1.7 copy-start.1
  94.6 3.3 copy-start.3
  98.0 1.9 copy-start.4
  103.2 1.2 copy-start.5
  103.2 1.5 copy-start.10
  371.3 4.5 %copy-start.11 = (f32[384,384]{1,0:T(8,128)S(1)}, f32[384,384]{1,0:T(8,128)}, u32[]{:S(2)}) copy-start(f32[384,384]{1,0:T(8,128)} %get-tuple-element.28) | copy-start | bytes 1769476
Sparse Core Ops, SparseCore 0:
  20.0 36.4 reduce-scatter.1
  105.9 265.3 all-reduce.3
where the time goes:
time: 384 us; the launch traced here: 383 us
  waiting for transfers between devices  218 us (57%)
  blocking collectives  74.6 us (19%)
  local copies, waits for them, and re-layouts  38.5 us (10%)
  matrix products  27.1 us (7%)
  between operations  14.4 us (4%)
  other arithmetic  6.41 us (2%)
  starting transfers between devices  4.55 us (1%)
    psum x1, waiting for transfers between devices, body(): lax.psum((g_in, g_gain, g_qkv, g_out, g_head), ('dp', 'frame'))  190 us
    psum x1, blocking collectives, body(): lax.psum((g_in, g_gain, g_qkv, g_out, g_head), ('dp', 'frame'))  74.6 us
    reduce_scatter x1, waiting for transfers between devices, body(): lax.psum_scatter(jnp.where(inside[:, None], picked, 0.0).astype(jnp.bfloa...  18.2 us
    all_to_all x1, waiting for transfers between devices, body(): lax.all_to_all(outgoing, 'frame', split_axis=0, concat_axis=1, tiled=True)  9.2 us
  transfers between devices with their start and end apart: 3, of which 3 were waited for; matrix products, arithmetic and copies ran while one was open for 3% of the time, Pallas kernels for 0%

commit v1 on v0

--- a/solution.py
+++ b/solution.py
@@ -128,7 +128,7 @@
         corr, cotangent[0], w_in, gain, w_qkv, w_out, w_head
     )
     s_in, s_gain, s_qkv, s_out, s_head = lax.psum(
-        (g_in, g_gain, g_qkv, g_out, g_head), ("dp", "frame")
+        lax.psum((g_in, g_gain, g_qkv, g_out, g_head), "frame"), "dp"
     )
     return (s_in, s_gain, s_qkv, s_out, s_head)
 

time: 384 us -> 349 us (0.909)
  waiting for transfers between devices: 218 us -> 178 us
  blocking collectives: 74.6 us -> 79.2 us
    psum x1 -> x2, waiting for transfers between devices: 190 us -> 150 us  [the longest x1 79.1 us: body(): lax.psum(lax.psum((g_in, g_gain, g_qkv, g_out, g_head), 'frame'), 'dp')]
    psum x1 -> x2, blocking collectives: 74.6 us -> 79.2 us  [the longest x1 65 us: body(): lax.psum(lax.psum((g_in, g_gain, g_qkv, g_out, g_head), 'frame'), 'dp')]
  transfers between devices with their start and end apart: 3 -> 4, of which waited for: 3 -> 4; matrix products, arithmetic and copies ran while one was open for 3% -> 4% of each run, Pallas kernels for 0% -> 0%
where the time goes in v1:
time: 349 us; the launch traced here: 348 us
  waiting for transfers between devices  178 us (51%)
  blocking collectives  79.2 us (23%)
  local copies, waits for them, and re-layouts  38.5 us (11%)
  matrix products  27.1 us (8%)
  between operations  14.1 us (4%)
  other arithmetic  6.41 us (2%)
  starting transfers between devices  4.59 us (1%)
    psum x1, waiting for transfers between devices, body(): lax.psum(lax.psum((g_in, g_gain, g_qkv, g_out, g_head), 'frame'), 'dp')  79.1 us
    psum x1, waiting for transfers between devices, body(): lax.psum((g_in, g_gain, g_qkv, g_out, g_head), 'frame')  71.3 us
    psum x1, blocking collectives, body(): lax.psum(lax.psum((g_in, g_gain, g_qkv, g_out, g_head), 'frame'), 'dp')  65 us
    reduce_scatter x1, waiting for transfers between devices, body(): lax.psum_scatter(jnp.where(inside[:, None], picked, 0.0).astype(jnp.bfloa...  18.2 us
    psum x1, blocking collectives, body(): lax.psum((g_in, g_gain, g_qkv, g_out, g_head), 'frame')  14.2 us
    all_to_all x1, waiting for transfers between devices, body(): lax.all_to_all(outgoing, 'frame', split_axis=0, concat_axis=1, tiled=True)  9.2 us
  transfers between devices with their start and end apart: 4, of which 4 were waited for; matrix products, arithmetic and copies ran while one was open for 4% of the time, Pallas kernels for 0%

profile of v1, /device:TPU:2, one launch (start us, length us, event | category | flops | bytes accessed | tf_op | source)
XLA Modules:
  0.0 347.8 jit_solution(14156932568979104859)
XLA Ops:
  9.7 1.9 broadcast_select_fusion
  11.7 4.5 %all-to-all-start = ((bf16[16,2,2,8192]{3,2,1,0:T(2,128)(2,1)}), bf16[16,2,2,8192]{3,2,1,0:T(2,128)(2,1)}, u32[]{:S(2)}, u32[]{:S(2)}) async-start(bf16[16,2,2,8192]{3,2,1,0:T(2,128)(2,1)} %broadcast_select_fusion), calls=%async_computation.1 | async-start | bytes 2097152 | tf_op jit(solution)/shard_map/all_to_all | solution.py:116
  16.3 1.9 gather_fusion
  23.0 9.2 %all-to-all-done = bf16[16,2,2,8192]{3,2,1,0:T(2,128)(2,1)} async-done(((bf16[16,2,2,8192]{3,2,1,0:T(2,128)(2,1)}), bf16[16,2,2,8192]{3,2,1,0:T(2,128)(2,1)}, u32[]{:S(2)}, u32[]{:S(2)}) %all-to-all-start) | async-done | bytes 1048608 | tf_op jit(solution)/shard_map/all_to_all | solution.py:116
  32.2 3.4 copy.29
  35.6 2.7 reshape.196
  38.3 18.2 %reduce-scatter.2.cloned.1.call-done = bf16[32,128]{1,0:T(8,128)(2,1)} async-done(((bf16[256,128]{1,0:T(8,128)(2,1)}), bf16[32,128]{1,0:T(8,128)(2,1)}) %reduce-scatter.2.cloned.1.call-update) | async-done | bytes 8208 | tf_op jit(solution)/shard_map/reduce_scatter | solution.py:102
  56.5 2.1 fusion.13
  59.5 3.1 convolution_convert_fusion
  62.7 5.3 %reshape.198 = bf16[32,16,3,8,48]{4,3,2,1,0:T(8,128)(2,1)} reshape(bf16[512,1152]{1,0:T(8,128)(2,1)} %convolution_convert_fusion) | data formatting | bytes 2359296 | tf_op jit(solution)/shard_map/reshape | solution.py:44
  67.9 3.7 %fusion.40 = (bf16[32,16,1,8,48]{4,3,2,1,0:T(8,128)(2,1)}, bf16[32,16,1,8,48]{4,3,2,1,0:T(8,128)(2,1)}, bf16[32,16,1,8,48]{4,3,2,1,0:T(8,128)(2,1)}) fusion(bf16[32,16,3,8,48]{4,3,2,1,0:T(8,128)(2,1)} %reshape.198), kind=kLoop, calls=%fused_computation.78 | loop fusion | bytes 2359296 | tf_op jit(solution)/shard_map/slice | solution.py:45
  71.6 3.8 %fusion.42 = (f32[32,8,16]{2,1,0:T(8,128)S(1)}, f32[32,8,16,16]{3,2,1,0:T(8,128)}) fusion(bf16[32,16,1,8,48]{4,3,2,1,0:T(8,128)(2,1)} %get-tuple-element.20, bf16[32,16,1,8,48]{4,3,2,1,0:T(8,128)(2,1)} %get-tuple-element.19), kind=kOutput, calls=%fused_computation.80 | convolution fusion | flops 6488079 | bytes 1064960 | tf_op jit(solution)/shard_map/jvp()/sub | solution.py:14
  75.4 2.3 convolution_convert_fusion.5
  81.7 2.5 fusion.8
  87.2 2.5 copy.39
  89.6 5.0 %reshape.199 = bf16[512,1152]{1,0:T(8,128)(2,1)} reshape(bf16[32,16,3,8,48]{4,3,2,1,0:T(8,128)(2,1)} %copy.39) | data formatting | bytes 2359296 | tf_op jit(solution)/shard_map/reshape | solution.py:57
  94.6 3.3 multiply_reduce_fusion.1
  98.0 1.9 fusion.37
  101.1 2.0 reshape.200
  105.8 71.3 %all-reduce.9.cloned.1.call-done = (f32[128,384]{1,0:T(8,128)}, f32[384,1152]{1,0:T(8,128)}, f32[384,384]{1,0:T(8,128)}) async-done(((f32[128,384]{1,0:T(8,128)}, f32[384,1152]{1,0:T(8,128)}, f32[384,384]{1,0:T(8,128)}), (f32[128,384]{1,0:T(8,128)}, f32[384,1152]{1,0:T(8,128)}, f32[384,384]{1,0:T(8,128)})) %all-reduce.9.cloned.1.call-update) | async-done | bytes 2555920 | tf_op jit(solution)/shard_map/psum | solution.py:131
  177.7 14.2 %all-reduce.2 = (f32[384]{0:T(512)S(1)}, f32[4,384]{1,0:T(4,128)S(1)}) all-reduce(f32[384]{0:T(512)S(1)} %get-tuple-element.5, f32[4,384]{1,0:T(4,128)S(1)} %fusion.14), channel_id=1, replica_groups=mesh['dp'=32,'frame'=8] {'frame'}, use_global_device_ids=true, to_apply=%region_11.12 | all-reduce | flops 1920 | bytes 15360 | tf_op jit(solution)/shard_map/psum | solution.py:131
  191.8 65.0 %all-reduce = (f32[384]{0:T(512)}, f32[4,384]{1,0:T(4,128)}) all-reduce(f32[384]{0:T(512)S(1)} %get-tuple-element.13, f32[4,384]{1,0:T(4,128)S(1)} %get-tuple-element.14), channel_id=1, replica_groups=mesh['dp'=32,'frame'=8] {'dp'}, use_global_device_ids=true, to_apply=%region_12.13 | all-reduce | flops 1920 | bytes 15360 | tf_op jit(solution)/shard_map/psum | solution.py:130
  256.9 79.1 %all-reduce.7.cloned.1.call-done = (f32[128,384]{1,0:T(8,128)}, f32[384,1152]{1,0:T(8,128)}, f32[384,384]{1,0:T(8,128)}) async-done(((f32[128,384]{1,0:T(8,128)}, f32[384,1152]{1,0:T(8,128)}, f32[384,384]{1,0:T(8,128)}), (f32[128,384]{1,0:T(8,128)}, f32[384,1152]{1,0:T(8,128)}, f32[384,384]{1,0:T(8,128)})) %all-reduce.7.cloned.1.call-update) | async-done | bytes 2555920 | tf_op jit(solution)/shard_map/psum | solution.py:130
  337.7 2.8 copy.89
  (82 shorter events, 21.9 us)
Async XLA Ops:
  7.2 1.2 copy-start
  8.4 1.1 copy-start.17
  9.7 6.5 %copy-start.15 = (s32[1,256]{1,0:T(1,128)S(1)}, s32[1,256]{1,0:T(1,128)}, u32[]{:S(2)}) copy-start(s32[1,256]{1,0:T(1,128)} %param.15) | copy-start | bytes 3076
  9.7 6.5 %copy-start.18 = (s32[1,256]{1,0:T(1,128)S(1)}, s32[1,256]{1,0:T(1,128)}, u32[]{:S(2)}) copy-start(s32[1,256]{1,0:T(1,128)} %param.17) | copy-start | bytes 3076
  9.7 6.5 %copy-start.19 = (s32[1,256]{1,0:T(1,128)S(1)}, s32[1,256]{1,0:T(1,128)}, u32[]{:S(2)}) copy-start(s32[1,256]{1,0:T(1,128)} %param.16) | copy-start | bytes 3076
  9.7 9.3 %copy-start.14 = (bf16[1,4,32,16]{2,3,1,0:T(8,128)(2,1)S(1)}, bf16[1,4,32,16]{2,3,1,0:T(8,128)(2,1)}, u32[]{:S(2)}) copy-start(bf16[1,4,32,16]{2,3,1,0:T(8,128)(2,1)} %param.18) | copy-start | bytes 12292
  9.7 9.5 %copy-start.16 = (bf16[4,384]{1,0:T(4,128)(2,1)S(1)}, bf16[4,384]{1,0:T(4,128)(2,1)}, u32[]{:S(2)}) copy-start(bf16[4,384]{1,0:T(4,128)(2,1)} %param.23) | copy-start | bytes 9220
  11.7 20.5 %all-to-all-start = ((bf16[16,2,2,8192]{3,2,1,0:T(2,128)(2,1)}), bf16[16,2,2,8192]{3,2,1,0:T(2,128)(2,1)}, u32[]{:S(2)}, u32[]{:S(2)}) async-start(bf16[16,2,2,8192]{3,2,1,0:T(2,128)(2,1)} %broadcast_select_fusion), calls=%async_computation.1 | async-start | bytes 2097152 | tf_op jit(solution)/shard_map/all_to_all | solution.py:116
  16.1 4.6 %copy-start.7 = (bf16[384,384]{1,0:T(8,128)(2,1)S(1)}, bf16[384,384]{1,0:T(8,128)(2,1)}, u32[]{:S(2)}) copy-start(bf16[384,384]{1,0:T(8,128)(2,1)} %param.22) | copy-start | bytes 884740
  16.1 40.4 %reduce-scatter.2.cloned.1.call-start = ((), (), s32[]{:S(2)}) async-start(), calls=%async_computation.2 | async-start | bytes 73728 | tf_op jit(solution)/shard_map/reduce_scatter | solution.py:102
  19.0 158.1 %all-reduce.9.cloned.1.call-start = ((), (), s32[]{:S(2)}) async-start(), calls=%async_computation.4 | async-start | bytes 5111808 | tf_op jit(solution)/shard_map/psum | solution.py:131
  35.6 23.4 %copy-start.12 = (bf16[128,384]{1,0:T(8,128)(2,1)S(1)}, bf16[128,384]{1,0:T(8,128)(2,1)}, u32[]{:S(2)}) copy-start(bf16[128,384]{1,0:T(8,128)(2,1)} %param.19) | copy-start | bytes 294916
  38.3 21.2 %copy-start.13 = (f32[384]{0:T(512)S(1)}, f32[384]{0:T(512)}, u32[]{:S(2)}) copy-start(f32[384]{0:T(512)} %param.20) | copy-start | bytes 4612
  75.4 2.4 copy-start.6
  77.8 1.9 copy-start.9
  79.7 1.9 copy-start.8
  81.7 2.5 copy-start.2
  84.2 1.7 copy-start.1
  94.6 3.3 copy-start.3
  98.0 1.9 copy-start.4
  103.2 1.2 copy-start.5
  103.2 1.5 copy-start.10
  105.8 230.3 %all-reduce.7.cloned.1.call-start = ((), (), s32[]{:S(2)}) async-start(), calls=%async_computation.3 | async-start | bytes 5111808 | tf_op jit(solution)/shard_map/psum | solution.py:130
  336.0 4.5 %copy-start.11 = (f32[384,384]{1,0:T(8,128)S(1)}, f32[384,384]{1,0:T(8,128)}, u32[]{:S(2)}) copy-start(f32[384,384]{1,0:T(8,128)} %get-tuple-element.33) | copy-start | bytes 1769476
Sparse Core Ops, SparseCore 0:
  20.0 36.4 reduce-scatter.1
  105.9 71.1 all-reduce.8
  180.9 155.0 all-reduce.6
